TPU v7x, 256 devices: a whole 4x4x8 slice. The times are simulated.
256 devices in a mesh: px: 32 (over z, x), py: 8 (over y, core).
Axes of the slice: x: 4, y: 4, z: 8, core: 2. Of those that a mesh axis runs over, the one named last changes fastest.
Arguments:
- field: float32 [512, 512, 1024], P('px', 'py'), may hold values from -120 to 120
- seeds_first: int32 [512, 128], replicated, may hold values from -64 to 63
- seeds_second: int32 [512, 128], replicated, may hold values from -64 to 63
Outputs:
- basis_first: float32 [512, 128], replicated
- basis_second: float32 [512, 128], replicated
- core_tensor: float32 [128, 128, 1024], P('px', 'py')
All inputs are finite; a program needn't handle non-finite values.
Results may differ from a plain program's by a relative error of at most 0.0003.
Values sent between devices are 32-bit elements; how exact they have to be, the bound alone decides.
No kernel may reach another device: no remote copies, remote signals or barrier semaphores. Data moves between devices by JAX's collectives and lax.ppermute only.
A program may use at most 128 MiB of HBM per device.

v0:
```python
import jax
import jax.numpy as jnp
from jax import lax
from jax.sharding import PartitionSpec as P

ITERS = 4


def orthonormal(matrix):
    inner = jnp.dot(matrix.T, matrix, precision=lax.Precision.HIGHEST)
    factor = jnp.linalg.cholesky(inner)
    return jax.scipy.linalg.solve_triangular(factor, matrix.T, lower=True).T


def leading_basis(partial_gram, seeds):
    basis = orthonormal(seeds.astype(jnp.float32))
    gram = lax.psum(partial_gram, ("px", "py"))
    for sweep in range(ITERS):
        basis = orthonormal(jnp.dot(gram, basis, precision=lax.Precision.HIGHEST))
    return basis


def local(field, seeds_first, seeds_second):
    fibers = lax.all_to_all(field, "px", split_axis=1, concat_axis=0, tiled=True)
    whole_first = fibers.shape[0]
    flattened = fibers.reshape(whole_first, -1)
    partial_first = jnp.dot(flattened, flattened.T, precision=lax.Precision.HIGHEST)
    basis_first = leading_basis(partial_first, seeds_first)
    rank_size = basis_first.shape[1]
    reduced = jnp.dot(basis_first.T, flattened, precision=lax.Precision.HIGHEST)
    reduced = reduced.reshape(rank_size, fibers.shape[1], fibers.shape[2])
    slab_fibers = lax.all_to_all(
        lax.all_to_all(reduced, "px", split_axis=0, concat_axis=1, tiled=True),
        "py",
        split_axis=2,
        concat_axis=1,
        tiled=True,
    )
    whole_second = slab_fibers.shape[1]
    turned = jnp.transpose(slab_fibers, (1, 0, 2)).reshape(whole_second, -1)
    partial_second = jnp.dot(turned, turned.T, precision=lax.Precision.HIGHEST)
    basis_second = leading_basis(partial_second, seeds_second)
    core_tensor = jnp.einsum(
        "jb,ajp->abp", basis_second, slab_fibers, precision=lax.Precision.HIGHEST
    )
    core_tensor = lax.all_to_all(core_tensor, "py", split_axis=1, concat_axis=2, tiled=True)
    return (basis_first, basis_second, core_tensor)


def solution(mesh):
    placed = (P("px", "py", None), P(), P())
    return jax.shard_map(
        local,
        mesh=mesh,
        in_specs=placed,
        out_specs=(P(), P(), P("px", "py", None)),
        check_vma=False,
    )
```

profile of v0, /device:TPU:1, one launch (start us, length us, event | category | flops | bytes accessed | tf_op | source)
XLA Modules:
  0.0 948.8 jit_solution(8441352326940024443)
XLA Ops:
  7.2 6.6 copy.84
  13.8 12.1 %all-to-all-start = ((f32[16,64,1024]{2,0,1:T(8,128)}), f32[16,64,1024]{2,0,1:T(8,128)}, u32[]{:S(2)}, u32[]{:S(2)}) async-start(f32[16,64,1024]{2,0,1:T(8,128)} %copy.84), calls=%async_computation | async-start | bytes 8388608 | tf_op jit(solution)/shard_map/all_to_all | solution.py:24
  27.0 11.7 %cholesky.164 = f32[128,128]{1,0:T(8,128)S(1)} custom-call(f32[128,128]{1,0:T(8,128)S(1)} %fusion.58), custom_call_target="Cholesky" | custom-call | tf_op jit(solution)/shard_map/jit(cholesky)/cholesky | solution.py:11
  38.7 80.2 %all-to-all-done = f32[16,64,1024]{2,0,1:T(8,128)} async-done(((f32[16,64,1024]{2,0,1:T(8,128)}), f32[16,64,1024]{2,0,1:T(8,128)}, u32[]{:S(2)}, u32[]{:S(2)}) %all-to-all-start) | async-done | bytes 4194336 | tf_op jit(solution)/shard_map/all_to_all | solution.py:24
  118.9 5.5 copy.85
  124.5 2.0 copy.112
  126.4 1.9 copy-done
  128.4 8.4 fusion.67
  138.1 9.8 %custom-call.14 = f32[1,128,128]{1,2,0:T(8,128)S(1)} custom-call(f32[1,128,128]{2,1,0:T(8,128)S(1)} %fusion.29), custom_call_target="InvertDiagBlocksLowerTriangular" | custom-call | tf_op jit(solution)/shard_map/jit(_solve_triangular)/triangular_solve | solution.py:12
  148.3 5.5 copy.91
  153.9 237.6 %all-reduce.3.cloned.1.call-done = f32[512,512]{1,0:T(8,128)} async-done(((f32[512,512]{1,0:T(8,128)}), f32[512,512]{1,0:T(8,128)}) %all-reduce.3.cloned.1.call-update) | async-done | bytes 1048592 | tf_op jit(solution)/shard_map/psum | solution.py:17
  391.5 2.3 fusion.68
  394.5 11.7 %cholesky.175 = f32[128,128]{1,0:T(8,128)S(1)} custom-call(f32[128,128]{1,0:T(8,128)S(1)} %fusion.56), custom_call_target="Cholesky" | custom-call | tf_op jit(solution)/shard_map/jit(cholesky)/cholesky | solution.py:11
  407.6 9.8 %custom-call.15 = f32[1,128,128]{1,2,0:T(8,128)S(1)} custom-call(f32[1,128,128]{2,1,0:T(8,128)S(1)} %fusion.30), custom_call_target="InvertDiagBlocksLowerTriangular" | custom-call | tf_op jit(solution)/shard_map/jit(_solve_triangular)/triangular_solve | solution.py:12
  417.8 2.2 fusion.70
  420.8 11.9 %cholesky.186 = f32[128,128]{1,0:T(8,128)S(1)} custom-call(f32[128,128]{1,0:T(8,128)S(1)} %fusion.54), custom_call_target="Cholesky" | custom-call | tf_op jit(solution)/shard_map/jit(cholesky)/cholesky | solution.py:11
  434.0 9.8 %custom-call.16 = f32[1,128,128]{1,2,0:T(8,128)S(1)} custom-call(f32[1,128,128]{2,1,0:T(8,128)S(1)} %fusion.31), custom_call_target="InvertDiagBlocksLowerTriangular" | custom-call | tf_op jit(solution)/shard_map/jit(_solve_triangular)/triangular_solve | solution.py:12
  444.3 1.0 fusion.72
  446.0 11.7 %cholesky.197 = f32[128,128]{1,0:T(8,128)S(1)} custom-call(f32[128,128]{1,0:T(8,128)S(1)} %fusion.52), custom_call_target="Cholesky" | custom-call | tf_op jit(solution)/shard_map/jit(cholesky)/cholesky | solution.py:11
  459.0 9.8 %custom-call.17 = f32[1,128,128]{1,2,0:T(8,128)S(1)} custom-call(f32[1,128,128]{2,1,0:T(8,128)S(1)} %fusion.32), custom_call_target="InvertDiagBlocksLowerTriangular" | custom-call | tf_op jit(solution)/shard_map/jit(_solve_triangular)/triangular_solve | solution.py:12
  469.2 1.4 fusion.74
  471.3 11.7 %cholesky.208 = f32[128,128]{1,0:T(8,128)S(1)} custom-call(f32[128,128]{1,0:T(8,128)S(1)} %fusion.50), custom_call_target="Cholesky" | custom-call | tf_op jit(solution)/shard_map/jit(cholesky)/cholesky | solution.py:11
  484.4 9.8 %custom-call.18 = f32[1,128,128]{1,2,0:T(8,128)S(1)} custom-call(f32[1,128,128]{2,1,0:T(8,128)S(1)} %fusion.33), custom_call_target="InvertDiagBlocksLowerTriangular" | custom-call | tf_op jit(solution)/shard_map/jit(_solve_triangular)/triangular_solve | solution.py:12
  494.6 6.5 fusion.11
  502.1 35.5 %all_to_all.69 = f32[128,2,1024]{2,1,0:T(2,128)S(1)} all-to-all(f32[128,2,1024]{2,1,0:T(2,128)S(1)} %copy.92), channel_id=1, replica_groups=mesh['px'=32,'py'=8] {'px'}, dimensions={0} | all-to-all | bytes 2097152 | tf_op jit(solution)/shard_map/all_to_all | solution.py:33
  539.0 2.8 reshape.25
  541.8 6.2 all-to-all-start.2
  548.8 11.7 %cholesky.219 = f32[128,128]{1,0:T(8,128)S(1)} custom-call(f32[128,128]{1,0:T(8,128)S(1)} %fusion.48), custom_call_target="Cholesky" | custom-call | tf_op jit(solution)/shard_map/jit(cholesky)/cholesky | solution.py:11
  560.5 2.6 all-to-all-done.2
  563.7 3.1 reduce.4
  566.8 1.4 reshape.26
  568.2 1.0 copy.110
  569.3 2.9 convolution_bitcast_fusion
  573.5 9.8 %custom-call.19 = f32[1,128,128]{1,2,0:T(8,128)S(1)} custom-call(f32[1,128,128]{2,1,0:T(8,128)S(1)} %fusion.34), custom_call_target="InvertDiagBlocksLowerTriangular" | custom-call | tf_op jit(solution)/shard_map/jit(_solve_triangular)/triangular_solve | solution.py:12
  583.8 238.5 %all-reduce.5.cloned.1.call-done = f32[512,512]{1,0:T(8,128)} async-done(((f32[512,512]{1,0:T(8,128)}), f32[512,512]{1,0:T(8,128)}) %all-reduce.5.cloned.1.call-update) | async-done | bytes 1048592 | tf_op jit(solution)/shard_map/psum | solution.py:17
  822.2 2.3 fusion.76
  825.2 11.7 %cholesky.230 = f32[128,128]{1,0:T(8,128)S(1)} custom-call(f32[128,128]{1,0:T(8,128)S(1)} %fusion.46), custom_call_target="Cholesky" | custom-call | tf_op jit(solution)/shard_map/jit(cholesky)/cholesky | solution.py:11
  838.3 10.2 %custom-call.20 = f32[1,128,128]{1,2,0:T(8,128)S(1)} custom-call(f32[1,128,128]{2,1,0:T(8,128)S(1)} %fusion.35), custom_call_target="InvertDiagBlocksLowerTriangular" | custom-call | tf_op jit(solution)/shard_map/jit(_solve_triangular)/triangular_solve | solution.py:12
  848.9 2.2 fusion.78
  851.8 11.7 %cholesky.241 = f32[128,128]{1,0:T(8,128)S(1)} custom-call(f32[128,128]{1,0:T(8,128)S(1)} %fusion.44), custom_call_target="Cholesky" | custom-call | tf_op jit(solution)/shard_map/jit(cholesky)/cholesky | solution.py:11
  864.9 9.8 %custom-call.21 = f32[1,128,128]{1,2,0:T(8,128)S(1)} custom-call(f32[1,128,128]{2,1,0:T(8,128)S(1)} %fusion.36), custom_call_target="InvertDiagBlocksLowerTriangular" | custom-call | tf_op jit(solution)/shard_map/jit(_solve_triangular)/triangular_solve | solution.py:12
  876.8 11.9 %cholesky.252 = f32[128,128]{1,0:T(8,128)S(1)} custom-call(f32[128,128]{1,0:T(8,128)S(1)} %fusion.42), custom_call_target="Cholesky" | custom-call | tf_op jit(solution)/shard_map/jit(cholesky)/cholesky | solution.py:11
  890.0 9.8 %custom-call.22 = f32[1,128,128]{1,2,0:T(8,128)S(1)} custom-call(f32[1,128,128]{2,1,0:T(8,128)S(1)} %fusion.37), custom_call_target="InvertDiagBlocksLowerTriangular" | custom-call | tf_op jit(solution)/shard_map/jit(_solve_triangular)/triangular_solve | solution.py:12
  902.0 11.7 %cholesky.263 = f32[128,128]{1,0:T(8,128)S(1)} custom-call(f32[128,128]{1,0:T(8,128)S(1)} %fusion.40), custom_call_target="Cholesky" | custom-call | tf_op jit(solution)/shard_map/jit(cholesky)/cholesky | solution.py:11
  915.0 10.0 %custom-call.23 = f32[1,128,128]{1,2,0:T(8,128)S(1)} custom-call(f32[1,128,128]{2,1,0:T(8,128)S(1)} %fusion.38), custom_call_target="InvertDiagBlocksLowerTriangular" | custom-call | tf_op jit(solution)/shard_map/jit(_solve_triangular)/triangular_solve | solution.py:12
  925.5 1.8 convolution_bitcast_fusion.1
  928.1 6.4 all-to-all-start.3
  936.1 4.8 all-to-all-done.3
  (96 shorter events, 32.8 us)
Async XLA Ops:
  13.8 12.5 %copy-start.3 = (s32[512,128]{1,0:T(8,128)S(1)}, s32[512,128]{1,0:T(8,128)}, u32[]{:S(2)}) copy-start(s32[512,128]{1,0:T(8,128)} %param.7) | copy-start | bytes 786436
  13.8 105.2 %all-to-all-start = ((f32[16,64,1024]{2,0,1:T(8,128)}), f32[16,64,1024]{2,0,1:T(8,128)}, u32[]{:S(2)}, u32[]{:S(2)}) async-start(f32[16,64,1024]{2,0,1:T(8,128)} %copy.84), calls=%async_computation | async-start | bytes 8388608 | tf_op jit(solution)/shard_map/all_to_all | solution.py:24
  25.9 365.6 %all-reduce.3.cloned.1.call-start = ((), (), s32[]{:S(2)}) async-start(), calls=%async_computation.4 | async-start | bytes 2097152 | tf_op jit(solution)/shard_map/psum | solution.py:17
  126.4 1.9 copy-start
  391.5 52.7 %copy-start.1 = (f32[512,512]{1,0:T(8,128)S(1)}, f32[512,512]{1,0:T(8,128)}, u32[]{:S(2)}) copy-start(f32[512,512]{1,0:T(8,128)} %all-reduce.3.cloned.1.call-done) | copy-start | bytes 3145732
  539.0 9.0 copy-start.4
  541.8 21.3 %all-to-all-start.2 = ((f32[8,1,32768]{2,1,0:T(1,128)}), f32[8,1,32768]{2,1,0:T(1,128)S(1)}, u32[]{:S(2)}, u32[]{:S(2)}) async-start(f32[8,1,32768]{2,1,0:T(1,128)} %reshape.25), calls=%async_computation.2 | async-start | bytes 2097152 | tf_op jit(solution)/shard_map/all_to_all | solution.py:32
  548.1 274.2 %all-reduce.5.cloned.1.call-start = ((), (), s32[]{:S(2)}) async-start(), calls=%async_computation.5 | async-start | bytes 2097152 | tf_op jit(solution)/shard_map/psum | solution.py:17
  569.3 14.1 %copy-start.5 = (s32[512,128]{1,0:T(8,128)S(1)}, s32[512,128]{1,0:T(8,128)}, u32[]{:S(2)}) copy-start(s32[512,128]{1,0:T(8,128)} %param.8) | copy-start | bytes 786436
  822.2 52.9 %copy-start.2 = (f32[512,512]{1,0:T(8,128)S(1)}, f32[512,512]{1,0:T(8,128)}, u32[]{:S(2)}) copy-start(f32[512,512]{1,0:T(8,128)} %all-reduce.5.cloned.1.call-done) | copy-start | bytes 3145732
  928.1 12.9 %all-to-all-start.3 = ((f32[4,128,128]{2,0,1:T(4,128)}), f32[4,128,128]{2,0,1:T(4,128)S(1)}, u32[]{:S(2)}, u32[]{:S(2)}) async-start(f32[4,128,128]{2,0,1:T(4,128)} %copy.103), calls=%async_computation.3 | async-start | bytes 524288 | tf_op jit(solution)/shard_map/all_to_all | solution.py:46
Sparse Core Ops, SparseCore 0:
  136.9 254.5 all-reduce.2
  572.3 249.8 all-reduce.4
where the time goes:
time: 952 us; the launch traced here: 949 us
  waiting for transfers between devices  564 us (59%)
  other arithmetic  233 us (24%)
  matrix products  43 us (5%)
  blocking collectives  35.5 us (4%)
  local copies, waits for them, and re-layouts  33.7 us (4%)
  starting transfers between devices  25.1 us (3%)
  between operations  14.9 us (2%)
    psum x2, waiting for transfers between devices, leading_basis(): gram = lax.psum(partial_gram, ('px', 'py'))  476 us
    another operation x30, other arithmetic, orthonormal(): factor = jnp.linalg.cholesky(inner)  124 us
    another operation x20, other arithmetic, orthonormal(): return jax.scipy.linalg.solve_triangular(factor, matrix.T, lower=True).T  105 us
    all_to_all x1, waiting for transfers between devices, local(): lax.all_to_all(field, 'px', split_axis=1, concat_axis=0, tiled=True)  80.2 us
    all_to_all x1, blocking collectives, local(): lax.all_to_all(reduced, 'px', split_axis=0, concat_axis=1, tiled=True)  35.5 us
  transfers between devices with their start and end apart: 5, of which 5 were waited for; matrix products, arithmetic and copies ran while one was open for 6% of the time, Pallas kernels for 0%

commit v1 on v0

--- a/solution.py
+++ b/solution.py
@@ -14,7 +14,7 @@
 
 def leading_basis(partial_gram, seeds):
     basis = orthonormal(seeds.astype(jnp.float32))
-    gram = lax.psum(partial_gram, ("px", "py"))
+    gram = jax.lax.psum(jax.lax.psum(partial_gram, "px"), "py")
     for sweep in range(ITERS):
         basis = orthonormal(jnp.dot(gram, basis, precision=lax.Precision.HIGHEST))
     return basis

time: 952 us -> 868 us (0.912)
  waiting for transfers between devices: 564 us -> 376 us
  blocking collectives: 35.5 us -> 163 us
  starting transfers between devices: 25.1 us -> 6.37 us
    all_to_all x0 -> x2, blocking collectives: none -> 129 us  [the longest x1 105 us: local(): lax.all_to_all(field, 'px', split_axis=1, concat_axis=0, tiled=True)]
    psum x2 -> x4, waiting for transfers between devices: 476 us -> 371 us  [leading_basis(): gram = jax.lax.psum(jax.lax.psum(partial_gram, 'px'), 'py')]
    all_to_all x2 -> x0, waiting for transfers between devices: 82.9 us -> none  [the longest x1 80.2 us: local(): lax.all_to_all(field, 'px', split_axis=1, concat_axis=0, tiled=True)]
    all_to_all x2 -> x0, starting transfers between devices: 18.4 us -> none  [the longest x1 12.1 us: local(): lax.all_to_all(field, 'px', split_axis=1, concat_axis=0, tiled=True)]
where the time goes in v1:
time: 868 us; the launch traced here: 864 us
  waiting for transfers between devices  376 us (43%)
  other arithmetic  233 us (27%)
  blocking collectives  163 us (19%)
  matrix products  43.1 us (5%)
  local copies, waits for them, and re-layouts  28.6 us (3%)
  between operations  14.8 us (2%)
    psum x4, waiting for transfers between devices, leading_basis(): gram = jax.lax.psum(jax.lax.psum(partial_gram, 'px'), 'py')  371 us
    another operation x30, other arithmetic, orthonormal(): factor = jnp.linalg.cholesky(inner)  125 us
    all_to_all x1, blocking collectives, local(): lax.all_to_all(field, 'px', split_axis=1, concat_axis=0, tiled=True)  105 us
    another operation x20, other arithmetic, orthonormal(): return jax.scipy.linalg.solve_triangular(factor, matrix.T, lower=True).T  105 us
    all_to_all x1, blocking collectives, local(): lax.all_to_all(reduced, 'px', split_axis=0, concat_axis=1, tiled=True)  33.9 us
    all_to_all x1, blocking collectives, local(): lax.all_to_all(lax.all_to_all(reduced, 'px', split_axis=0, concat_axis=1,...  24.1 us
  transfers between devices with their start and end apart: 5, of which 5 were waited for; matrix products, arithmetic and copies ran while one was open for 6% of the time, Pallas kernels for 0%

profile of v1, /device:TPU:1, one launch (start us, length us, event | category | flops | bytes accessed | tf_op | source)
XLA Modules:
  0.0 864.5 jit_solution(15549265519671015609)
XLA Ops:
  7.2 4.6 copy.84
  11.8 105.3 %all_to_all.69 = f32[16,64,1024]{2,0,1:T(8,128)S(1)} all-to-all(f32[16,64,1024]{2,0,1:T(8,128)S(1)} %copy.84), channel_id=1, replica_groups=mesh['px'=32,'py'=8] {'px'}, dimensions={1} | all-to-all | bytes 8388608 | tf_op jit(solution)/shard_map/all_to_all | solution.py:24
  117.1 3.4 copy.85
  120.5 2.0 copy.112
  122.5 1.9 copy-done
  124.4 8.4 fusion.67
  133.6 11.7 %cholesky.164 = f32[128,128]{1,0:T(8,128)S(1)} custom-call(f32[128,128]{1,0:T(8,128)S(1)} %fusion.58), custom_call_target="Cholesky" | custom-call | tf_op jit(solution)/shard_map/jit(cholesky)/cholesky | solution.py:11
  145.4 131.9 %all-reduce.5.cloned.1.call-done = f32[512,512]{1,0:T(8,128)} async-done(((f32[512,512]{1,0:T(8,128)}), f32[512,512]{1,0:T(8,128)}) %all-reduce.5.cloned.1.call-update) | async-done | bytes 1048592 | tf_op jit(solution)/shard_map/psum | solution.py:17
  278.6 9.8 %custom-call.14 = f32[1,128,128]{1,2,0:T(8,128)S(1)} custom-call(f32[1,128,128]{2,1,0:T(8,128)S(1)} %fusion.29), custom_call_target="InvertDiagBlocksLowerTriangular" | custom-call | tf_op jit(solution)/shard_map/jit(_solve_triangular)/triangular_solve | solution.py:12
  288.9 5.5 copy.91
  294.4 52.9 %all-reduce.7.cloned.1.call-done = f32[512,512]{1,0:T(8,128)} async-done(((f32[512,512]{1,0:T(8,128)}), f32[512,512]{1,0:T(8,128)}) %all-reduce.7.cloned.1.call-update) | async-done | bytes 1048592 | tf_op jit(solution)/shard_map/psum | solution.py:17
  347.2 2.3 fusion.68
  350.3 11.7 %cholesky.175 = f32[128,128]{1,0:T(8,128)S(1)} custom-call(f32[128,128]{1,0:T(8,128)S(1)} %fusion.56), custom_call_target="Cholesky" | custom-call | tf_op jit(solution)/shard_map/jit(cholesky)/cholesky | solution.py:11
  363.3 9.8 %custom-call.15 = f32[1,128,128]{1,2,0:T(8,128)S(1)} custom-call(f32[1,128,128]{2,1,0:T(8,128)S(1)} %fusion.30), custom_call_target="InvertDiagBlocksLowerTriangular" | custom-call | tf_op jit(solution)/shard_map/jit(_solve_triangular)/triangular_solve | solution.py:12
  373.6 2.2 fusion.70
  376.5 11.9 %cholesky.186 = f32[128,128]{1,0:T(8,128)S(1)} custom-call(f32[128,128]{1,0:T(8,128)S(1)} %fusion.54), custom_call_target="Cholesky" | custom-call | tf_op jit(solution)/shard_map/jit(cholesky)/cholesky | solution.py:11
  389.7 9.8 %custom-call.16 = f32[1,128,128]{1,2,0:T(8,128)S(1)} custom-call(f32[1,128,128]{2,1,0:T(8,128)S(1)} %fusion.31), custom_call_target="InvertDiagBlocksLowerTriangular" | custom-call | tf_op jit(solution)/shard_map/jit(_solve_triangular)/triangular_solve | solution.py:12
  400.0 1.0 fusion.72
  401.7 11.7 %cholesky.197 = f32[128,128]{1,0:T(8,128)S(1)} custom-call(f32[128,128]{1,0:T(8,128)S(1)} %fusion.52), custom_call_target="Cholesky" | custom-call | tf_op jit(solution)/shard_map/jit(cholesky)/cholesky | solution.py:11
  414.7 9.8 %custom-call.17 = f32[1,128,128]{1,2,0:T(8,128)S(1)} custom-call(f32[1,128,128]{2,1,0:T(8,128)S(1)} %fusion.32), custom_call_target="InvertDiagBlocksLowerTriangular" | custom-call | tf_op jit(solution)/shard_map/jit(_solve_triangular)/triangular_solve | solution.py:12
  425.0 1.4 fusion.74
  427.1 11.7 %cholesky.208 = f32[128,128]{1,0:T(8,128)S(1)} custom-call(f32[128,128]{1,0:T(8,128)S(1)} %fusion.50), custom_call_target="Cholesky" | custom-call | tf_op jit(solution)/shard_map/jit(cholesky)/cholesky | solution.py:11
  440.1 9.8 %custom-call.18 = f32[1,128,128]{1,2,0:T(8,128)S(1)} custom-call(f32[1,128,128]{2,1,0:T(8,128)S(1)} %fusion.33), custom_call_target="InvertDiagBlocksLowerTriangular" | custom-call | tf_op jit(solution)/shard_map/jit(_solve_triangular)/triangular_solve | solution.py:12
  450.4 6.5 fusion.11
  457.9 33.9 %all_to_all.70 = f32[128,2,1024]{2,1,0:T(2,128)S(1)} all-to-all(f32[128,2,1024]{2,1,0:T(2,128)S(1)} %copy.92), channel_id=1, replica_groups=mesh['px'=32,'py'=8] {'px'}, dimensions={0} | all-to-all | bytes 2097152 | tf_op jit(solution)/shard_map/all_to_all | solution.py:33
  493.1 2.0 reshape.25
  495.1 24.1 %all_to_all.71 = f32[8,1,32768]{2,1,0:T(1,128)S(1)} all-to-all(f32[8,1,32768]{2,1,0:T(1,128)S(1)} %reshape.25), channel_id=1, replica_groups=mesh['px'=32,'py'=8] {'py'}, dimensions={0} | all-to-all | bytes 2097152 | tf_op jit(solution)/shard_map/all_to_all | solution.py:32
  519.6 3.1 reduce.4
  522.8 1.4 reshape.26
  525.0 2.9 convolution_bitcast_fusion
  528.9 11.7 %cholesky.219 = f32[128,128]{1,0:T(8,128)S(1)} custom-call(f32[128,128]{1,0:T(8,128)S(1)} %fusion.48), custom_call_target="Cholesky" | custom-call | tf_op jit(solution)/shard_map/jit(cholesky)/cholesky | solution.py:11
  540.7 128.0 %all-reduce.9.cloned.1.call-done = f32[512,512]{1,0:T(8,128)} async-done(((f32[512,512]{1,0:T(8,128)}), f32[512,512]{1,0:T(8,128)}) %all-reduce.9.cloned.1.call-update) | async-done | bytes 1048592 | tf_op jit(solution)/shard_map/psum | solution.py:17
  670.0 9.8 %custom-call.19 = f32[1,128,128]{1,2,0:T(8,128)S(1)} custom-call(f32[1,128,128]{2,1,0:T(8,128)S(1)} %fusion.34), custom_call_target="InvertDiagBlocksLowerTriangular" | custom-call | tf_op jit(solution)/shard_map/jit(_solve_triangular)/triangular_solve | solution.py:12
  680.2 58.3 %all-reduce.11.cloned.1.call-done = f32[512,512]{1,0:T(8,128)} async-done(((f32[512,512]{1,0:T(8,128)}), f32[512,512]{1,0:T(8,128)}) %all-reduce.11.cloned.1.call-update) | async-done | bytes 1048592 | tf_op jit(solution)/shard_map/psum | solution.py:17
  738.5 2.3 fusion.76
  741.6 12.1 %cholesky.230 = f32[128,128]{1,0:T(8,128)S(1)} custom-call(f32[128,128]{1,0:T(8,128)S(1)} %fusion.46), custom_call_target="Cholesky" | custom-call | tf_op jit(solution)/shard_map/jit(cholesky)/cholesky | solution.py:11
  755.0 9.8 %custom-call.20 = f32[1,128,128]{1,2,0:T(8,128)S(1)} custom-call(f32[1,128,128]{2,1,0:T(8,128)S(1)} %fusion.35), custom_call_target="InvertDiagBlocksLowerTriangular" | custom-call | tf_op jit(solution)/shard_map/jit(_solve_triangular)/triangular_solve | solution.py:12
  765.2 2.2 fusion.78
  768.2 11.7 %cholesky.241 = f32[128,128]{1,0:T(8,128)S(1)} custom-call(f32[128,128]{1,0:T(8,128)S(1)} %fusion.44), custom_call_target="Cholesky" | custom-call | tf_op jit(solution)/shard_map/jit(cholesky)/cholesky | solution.py:11
  781.2 9.8 %custom-call.21 = f32[1,128,128]{1,2,0:T(8,128)S(1)} custom-call(f32[1,128,128]{2,1,0:T(8,128)S(1)} %fusion.36), custom_call_target="InvertDiagBlocksLowerTriangular" | custom-call | tf_op jit(solution)/shard_map/jit(_solve_triangular)/triangular_solve | solution.py:12
  793.3 11.7 %cholesky.252 = f32[128,128]{1,0:T(8,128)S(1)} custom-call(f32[128,128]{1,0:T(8,128)S(1)} %fusion.42), custom_call_target="Cholesky" | custom-call | tf_op jit(solution)/shard_map/jit(cholesky)/cholesky | solution.py:11
  806.4 9.8 %custom-call.22 = f32[1,128,128]{1,2,0:T(8,128)S(1)} custom-call(f32[1,128,128]{2,1,0:T(8,128)S(1)} %fusion.37), custom_call_target="InvertDiagBlocksLowerTriangular" | custom-call | tf_op jit(solution)/shard_map/jit(_solve_triangular)/triangular_solve | solution.py:12
  816.6 1.0 fusion.82
  818.3 11.9 %cholesky.263 = f32[128,128]{1,0:T(8,128)S(1)} custom-call(f32[128,128]{1,0:T(8,128)S(1)} %fusion.40), custom_call_target="Cholesky" | custom-call | tf_op jit(solution)/shard_map/jit(cholesky)/cholesky | solution.py:11
  831.6 9.8 %custom-call.23 = f32[1,128,128]{1,2,0:T(8,128)S(1)} custom-call(f32[1,128,128]{2,1,0:T(8,128)S(1)} %fusion.38), custom_call_target="InvertDiagBlocksLowerTriangular" | custom-call | tf_op jit(solution)/shard_map/jit(_solve_triangular)/triangular_solve | solution.py:12
  841.8 1.8 convolution_bitcast_fusion.1
  844.4 6.0 all-to-all-start.3
  852.1 4.9 all-to-all-done.3
  (98 shorter events, 32.7 us)
Async XLA Ops:
  7.2 270.1 %all-reduce.5.cloned.1.call-start = ((), (), s32[]{:S(2)}) async-start(), calls=%async_computation.4 | async-start | bytes 2097152 | tf_op jit(solution)/shard_map/psum | solution.py:17
  122.5 1.9 copy-start
  124.4 8.5 copy-start.3
  132.8 214.4 %all-reduce.7.cloned.1.call-start = ((), (), s32[]{:S(2)}) async-start(), calls=%async_computation.5 | async-start | bytes 2097152 | tf_op jit(solution)/shard_map/psum | solution.py:17
  277.3 391.4 %all-reduce.9.cloned.1.call-start = ((), (), s32[]{:S(2)}) async-start(), calls=%async_computation.6 | async-start | bytes 2097152 | tf_op jit(solution)/shard_map/psum | solution.py:17
  347.2 52.7 %copy-start.1 = (f32[512,512]{1,0:T(8,128)S(1)}, f32[512,512]{1,0:T(8,128)}, u32[]{:S(2)}) copy-start(f32[512,512]{1,0:T(8,128)} %all-reduce.7.cloned.1.call-done) | copy-start | bytes 3145732
  525.0 3.2 copy-start.4
  528.0 210.6 %all-reduce.11.cloned.1.call-start = ((), (), s32[]{:S(2)}) async-start(), calls=%async_computation.7 | async-start | bytes 2097152 | tf_op jit(solution)/shard_map/psum | solution.py:17
  738.5 52.9 %copy-start.2 = (f32[512,512]{1,0:T(8,128)S(1)}, f32[512,512]{1,0:T(8,128)}, u32[]{:S(2)}) copy-start(f32[512,512]{1,0:T(8,128)} %all-reduce.11.cloned.1.call-done) | copy-start | bytes 3145732
  844.4 12.5 %all-to-all-start.3 = ((f32[4,128,128]{2,0,1:T(4,128)}), f32[4,128,128]{2,0,1:T(4,128)S(1)}, u32[]{:S(2)}, u32[]{:S(2)}) async-start(f32[4,128,128]{2,0,1:T(4,128)} %copy.103), calls=%async_computation.3 | async-start | bytes 524288 | tf_op jit(solution)/shard_map/all_to_all | solution.py:46
Sparse Core Ops, SparseCore 0:
  133.0 144.2 all-reduce.4
  279.6 67.5 all-reduce.6
  528.1 140.5 all-reduce.8
  670.9 67.5 all-reduce.10
